TPU v7x, 256 devices: a whole 4x4x8 slice. The times are simulated.
256 devices in a mesh: scan: 8 (over y_hi, x), cross: 32 (over y_lo, z, core).
Axes of the slice: x: 4, y: 4 (y_hi: 2, y_lo: 2; y = y_hi * 2 + y_lo), z: 8, core: 2. Of those that a mesh axis runs over, the one named last changes fastest.
Arguments:
- wafer_state: float32 [128, 512, 384], P('scan', 'cross'), may hold values from 0 to 1, as said below
- layer_heat_coefficients: float32 [256], replicated, may hold values from 0.03 to 0.14
- beam_profile: float32 [512], replicated, may hold values from 0.25 to 1.75
- beam_start: int32 [4], replicated, may hold values from 0 to 127
- beam_steps: int32 [4], replicated, may hold values from 1 to 64
Outputs:
- annealed: float32 [128, 512, 384], P('scan', 'cross')
Inputs may be any that keep to these rules, and one draw needn't show every extreme that they name: `wafer_state`: temperatures lie in 0 to 0.6, acid in 0 to 1, protection in 0.5 to 1.
All inputs are finite; a program needn't handle non-finite values.
Results may differ from a plain program's by a relative error of at most 0.00002.
Values sent between devices are 32-bit elements; how exact they have to be, the bound alone decides.
A program may use at most 64 MiB of HBM per device.

v0:
```python
import jax
import jax.numpy as jnp
from jax import lax
from jax.experimental import pallas as pl
from jax.experimental.pallas import tpu as pltpu
from jax.sharding import PartitionSpec as P

STEPS = 4
SUBSTEPS = 2
LEVELS = STEPS * SUBSTEPS
HALO = LEVELS
MESH = pl.DeviceIdType.MESH

heat_power = 0.5
absorb_depth = 6.0
barrier_energy = 3.0
frequency_multiplier = 0.6
proton_mobility = 0.15


def lane_roll(v, shift):
    return pltpu.roll(v, shift % v.shape[1], axis=1)


def sub_roll(v, shift):
    return pltpu.roll(v, shift % v.shape[0], axis=0)


def kernel(
    profile_ref, start_ref, steps_ref, coef_ref, x_ref, o_ref,
    st, qb, db, pb, spot, pa, send_sems, recv_sems, own_sem, out_sems, got_sems,
):
    s = lax.axis_index("scan")
    c = lax.axis_index("cross")
    n_scan = lax.axis_size("scan")
    n_cross = lax.axis_size("cross")
    rows = x_ref.shape[0]
    cols = x_ref.shape[1]
    total_x = rows * n_scan
    target = (lax.rem(s + n_scan - STEPS, n_scan), c)
    source = (lax.rem(s + STEPS, n_scan), c)
    f32 = jnp.float32

    barrier = pltpu.get_barrier_semaphore()
    sides = [(ds, dc) for dc in (-1, 1, 0) for ds in (0, -1, 1) if (ds, dc) != (0, 0)]

    def peer(ds, dc):
        return (lax.rem(s + ds + n_scan, n_scan), c + dc)

    def exists(dc):
        if dc < 0:
            return c > 0
        if dc > 0:
            return c < n_cross - 1
        return None

    def guarded(dc, fn):
        cond = exists(dc)
        if cond is None:
            fn()
        else:
            pl.when(cond)(fn)

    for ds, dc in sides:
        def greet(ds=ds, dc=dc):
            pl.semaphore_signal(barrier, 1, device_id=peer(ds, dc), device_id_type=MESH)
        guarded(dc, greet)
    pl.semaphore_signal(barrier, 1, device_id=target, device_id_type=MESH)

    own = pltpu.make_async_copy(
        x_ref, st.at[0, pl.ds(HALO, rows), pl.ds(HALO, cols), :], own_sem
    )
    own.start()

    edges = jnp.where(c > 0, 1, 0) + jnp.where(c < n_cross - 1, 1, 0)
    pl.semaphore_wait(barrier, 3 + 3 * edges)

    def span(d, length, sending):
        if d == 0:
            return pl.ds(0 if sending else HALO, length)
        if d > 0:
            return pl.ds(length - HALO if sending else 0, HALO)
        return pl.ds(0 if sending else HALO + length, HALO)

    copies = {}
    for k, (ds, dc) in enumerate(sides):
        copies[(ds, dc)] = pltpu.make_async_remote_copy(
            src_ref=x_ref.at[span(ds, rows, True), span(dc, cols, True), :],
            dst_ref=st.at[0, span(ds, rows, False), span(dc, cols, False), :],
            send_sem=send_sems.at[k],
            recv_sem=recv_sems.at[k],
            device_id=peer(ds, dc),
            device_id_type=MESH,
        )
    for ds, dc in sides:
        guarded(dc, copies[(ds, dc)].start)

    lane = lax.broadcasted_iota(jnp.int32, (8, 128), 1)
    sub = lax.broadcasted_iota(jnp.int32, (8, 128), 0)
    low = lane < 64
    low_f = jnp.where(low, 1.0, 0.0).astype(f32)
    last_sub = sub == 7
    first_sub = sub == 0
    last_lane = lane == 127
    first_lane = lane == 0
    inner_a = jnp.where(lane < 63, 1.0, 0.0).astype(f32)
    half_coef = [
        jnp.broadcast_to((0.5 * coef_ref[pl.ds(128 * h, 128)])[None, :], (8, 128)) for h in range(2)
    ]
    floor_coef = half_coef[1]

    for t in range(1, LEVELS + 1):
        f = (t - 1) // SUBSTEPS
        n = (t - 1) % SUBSTEPS
        center = (start_ref[f] + n * steps_ref[f]).astype(f32)
        for g in range(4):
            at = sub + (8 * g - HALO) + (s * rows - rows * f + 2 * total_x)
            where_x = lax.rem(at, jnp.int32(total_x)).astype(f32)
            ratio = (where_x - center) * (1.0 / float(rows // 2))
            spot[pl.ds((t - 1) * 32 + 8 * g, 8), :] = jnp.exp(-ratio * ratio)

    z0 = lane.astype(f32)
    absorb = [
        jnp.where(z0 + (128.0 * h) >= 64.0, jnp.exp(-(z0 + (128.0 * h - 64.0)) / absorb_depth), 0.0)
        for h in range(2)
    ]
    for j in range(4):
        col = jnp.zeros((8, 128), f32)
        for i in range(8):
            place = c * cols - HALO + 8 * j + i
            place = jnp.clip(place, 0, n_cross * cols - 1)
            col = jnp.where(sub == i, profile_ref[place], col)
        for h in range(2):
            pa[h, pl.ds(8 * j, 8), :] = heat_power * col * absorb[h]

    left_f = jnp.where(c > 0, 1.0, 0.0).astype(f32)
    right_f = jnp.where(c < n_cross - 1, 1.0, 0.0).astype(f32)
    edge_f = [left_f, None, None, right_f]

    def coupling(t0, t1):
        s0 = t0 * t0
        s1 = t1 * t1
        a = 1.0 + 0.25 * s0
        b = 1.0 + s0
        w = 1.0 / (a * b)
        q0 = b * w
        q1 = 1.0 / (1.0 + 0.25 * s1)
        d = (0.5 * proton_mobility) * s0 * (a * w) * low_f
        return q0, q1, d

    def tile(j):
        return pl.ds(8 * j, 8)

    def init_rows(first, count):
        def body(i, carry):
            X = first + HALO + i
            for j in range(4):
                q0, q1, d = coupling(
                    st[0, X, tile(j), pl.ds(0, 128)], st[0, X, tile(j), pl.ds(128, 128)]
                )
                qb[0, X, tile(j), pl.ds(0, 128)] = q0
                qb[0, X, tile(j), pl.ds(128, 128)] = q1
                db[0, X, tile(j), :] = d
            return carry

        lax.fori_loop(0, count, body, 0)

    def up(tiles):
        rolled = [sub_roll(v, -1) for v in tiles]
        return [
            jnp.where(last_sub, rolled[j + 1], rolled[j]) if j < 3 else rolled[j] for j in range(4)
        ]

    def down(tiles):
        rolled = [sub_roll(v, 1) for v in tiles]
        return [
            jnp.where(first_sub, rolled[j - 1] if j > 0 else 0.0, rolled[j]) for j in range(4)
        ]

    def y_net(vals, facs):
        vu = up(vals)
        fu = up(facs)
        flux = [(facs[j] + fu[j]) * (vu[j] - vals[j]) for j in range(4)]
        flux[3] = jnp.where(last_sub, 0.0, flux[3])
        prev = down(flux)
        return [flux[j] - prev[j] for j in range(4)]

    def block(t, r0):
        a = lax.rem(t + 1, 2)
        b = lax.rem(t, 2)
        X0 = r0 + HALO
        T = {}
        Q = {}
        A = {}
        D = {}
        for i in range(-1, 3):
            for j in range(4):
                for h in range(2):
                    T[i, j, h] = st[a, X0 + i, tile(j), pl.ds(128 * h, 128)]
                    Q[i, j, h] = qb[a, X0 + i, tile(j), pl.ds(128 * h, 128)]
                A[i, j] = st[a, X0 + i, tile(j), pl.ds(256, 128)]
                D[i, j] = db[a, X0 + i, tile(j), :]
        for i in range(2):
            r = r0 + i
            frame = lax.div(t, 2) - 1
            owner = lax.rem(s + lax.div(r + rows, rows) - 1 + n_scan, n_scan)
            wiped = jnp.logical_and(lax.rem(t, 2) == 0, owner == frame)
            keep = jnp.where(wiped, 0.0, 1.0).astype(f32)
            beam = jnp.broadcast_to(spot[pl.ds((t - 1) * 32 + X0 + i, 1), :], (8, 128))
            new = {}
            yn = [
                y_net([T[i, j, h] for j in range(4)], [Q[i, j, h] for j in range(4)])
                for h in range(2)
            ]
            for j in range(4):
                kz = [half_coef[h] * Q[i, j, h] for h in range(2)]
                tr = [lane_roll(T[i, j, h], -1) for h in range(2)]
                kr = [lane_roll(kz[h], -1) for h in range(2)]
                tn = [jnp.where(last_lane, tr[1], tr[0]), jnp.where(last_lane, 0.0, tr[1])]
                kn = [jnp.where(last_lane, kr[1], kr[0]), jnp.where(last_lane, floor_coef, kr[1])]
                fz = [(kz[h] + kn[h]) * (tn[h] - T[i, j, h]) for h in range(2)]
                fr = [lane_roll(fz[h], 1) for h in range(2)]
                fp = [jnp.where(first_lane, 0.0, fr[0]), jnp.where(first_lane, fr[0], fr[1])]
                for h in range(2):
                    cur = T[i, j, h]
                    fx1 = (Q[i, j, h] + Q[i + 1, j, h]) * (T[i + 1, j, h] - cur)
                    fx0 = (Q[i, j, h] + Q[i - 1, j, h]) * (cur - T[i - 1, j, h])
                    lateral = (fx1 - fx0) + yn[h][j]
                    value = cur + (half_coef[h] * lateral + (fz[h] - fp[h]))
                    value = value + beam * pa[h, tile(j), :]
                    scale = keep if edge_f[j] is None else keep * edge_f[j]
                    value = value * scale
                    new[j, h] = value
                    st[b, X0 + i, tile(j), pl.ds(128 * h, 128)] = value
                q0, q1, d = coupling(new[j, 0], new[j, 1])
                qb[b, X0 + i, tile(j), pl.ds(0, 128)] = q0
                qb[b, X0 + i, tile(j), pl.ds(128, 128)] = q1
                db[b, X0 + i, tile(j), :] = d
            ya = y_net([A[i, j] for j in range(4)], [D[i, j] for j in range(4)])
            for j in range(4):
                cur = A[i, j]
                an = lane_roll(cur, -1)
                dn = lane_roll(D[i, j], -1)
                fz = (D[i, j] + dn) * (an - cur) * inner_a
                fx1 = (D[i, j] + D[i + 1, j]) * (A[i + 1, j] - cur)
                fx0 = (D[i, j] + D[i - 1, j]) * (cur - A[i - 1, j])
                value = cur + ((fx1 - fx0) + ya[j] + (fz - lane_roll(fz, 1)))
                if edge_f[j] is not None:
                    value = value * edge_f[j]
                st[b, X0 + i, tile(j), pl.ds(256, 128)] = value

            @pl.when(jnp.logical_and(r >= 0, r < rows))
            def _(i=i, r=r):
                tp = jnp.where(low, T[i, 1, 0], lane_roll(T[i, 2, 0], 64))
                ap = jnp.where(low, A[i, 1], lane_roll(A[i, 2], 64))
                rate = frequency_multiplier * jnp.exp(-barrier_energy / (1.0 + tp))
                pb[r] = pb[r] * (1.0 - rate * ap)

    def march(first_of, count_of, levels):
        def level(t, carry):
            def pair(i, carry):
                block(t, first_of(t) + 2 * i)
                return carry

            lax.fori_loop(0, count_of(t), pair, 0)
            return carry

        lax.fori_loop(1, levels + 1, level, 0)

    def unpack(first, count):
        def body(i, carry):
            X = first + HALO + i
            packed = pb[first + i]
            turned = lane_roll(packed, 64)
            st[0, X, tile(1), pl.ds(256, 128)] = jnp.where(
                low, st[0, X, tile(1), pl.ds(256, 128)], turned
            )
            st[0, X, tile(2), pl.ds(256, 128)] = jnp.where(
                low, st[0, X, tile(2), pl.ds(256, 128)], packed
            )
            return carry

        lax.fori_loop(0, count, body, 0)

    own.wait()

    def pack(i, carry):
        X = HALO + i
        pb[i] = jnp.where(
            low,
            lane_roll(st[0, X, tile(1), pl.ds(256, 128)], 64),
            st[0, X, tile(2), pl.ds(256, 128)],
        )
        return carry

    lax.fori_loop(0, rows, pack, 0)

    def clear(j):
        def body(X, carry):
            for h in range(3):
                st[0, X, tile(j), pl.ds(128 * h, 128)] = jnp.zeros((8, 128), f32)
            return carry

        lax.fori_loop(0, rows + 2 * HALO, body, 0)

    pl.when(c == 0)(lambda: clear(0))
    pl.when(c == n_cross - 1)(lambda: clear(3))

    def arrive(ds):
        for dc in (-1, 0, 1):
            if (ds, dc) != (0, 0):
                k = sides.index((-ds, -dc))
                wait = pltpu.make_async_remote_copy(
                    src_ref=x_ref.at[span(-ds, rows, True), span(-dc, cols, True), :],
                    dst_ref=st.at[0, span(-ds, rows, False), span(-dc, cols, False), :],
                    send_sem=send_sems.at[k],
                    recv_sem=recv_sems.at[k],
                    device_id=peer(ds, dc),
                    device_id_type=MESH,
                )
                guarded(dc, wait.wait_recv)

    def out_copy(part):
        return pltpu.make_async_remote_copy(
            src_ref=st.at[0, pl.ds(HALO + 4 * part, 4), pl.ds(HALO, cols), :],
            dst_ref=o_ref.at[pl.ds(4 * part, 4)],
            send_sem=out_sems.at[part],
            recv_sem=got_sems.at[part],
            device_id=target,
            device_id_type=MESH,
        )

    arrive(0)
    init_rows(0, rows)
    march(lambda t: t, lambda t: 8 - t, LEVELS - 1)
    arrive(-1)
    for part, first in ((1, -4), (0, -8)):
        init_rows(first, 4)
        march(lambda t, first=first: t + first, lambda t: 2, LEVELS)
        unpack(4 * part, 4)
        out_copy(part).start()
    arrive(1)
    for part, first in ((2, 16), (3, 20)):
        init_rows(first, 4)
        march(lambda t, first=first: first - t, lambda t: 2, LEVELS)
        unpack(4 * part, 4)
        out_copy(part).start()
    for part in range(4):
        out_copy(part).wait()
    for ds, dc in sides:
        guarded(dc, copies[(ds, dc)].wait_send)


def shards(wafer_state, layer_heat_coefficients, beam_profile, beam_start, beam_steps):
    smem = pl.BlockSpec(memory_space=pltpu.SMEM)
    f32 = jnp.float32
    rows, cols, chans = wafer_state.shape
    X = rows + 2 * HALO
    Y = cols + 2 * HALO
    return pl.pallas_call(
        kernel,
        out_shape=jax.ShapeDtypeStruct(wafer_state.shape, f32),
        in_specs=[smem, smem, smem, pl.BlockSpec(memory_space=pltpu.VMEM), pl.BlockSpec(memory_space=pl.ANY)],
        out_specs=pl.BlockSpec(memory_space=pl.ANY),
        scratch_shapes=[
            pltpu.VMEM((2, X, Y, chans), f32),
            pltpu.VMEM((2, X, Y, 256), f32),
            pltpu.VMEM((2, X, Y, 128), f32),
            pltpu.VMEM((rows, 8, 128), f32),
            pltpu.VMEM((LEVELS * X, 128), f32),
            pltpu.VMEM((2, Y, 128), f32),
            pltpu.SemaphoreType.DMA((8,)),
            pltpu.SemaphoreType.DMA((8,)),
            pltpu.SemaphoreType.DMA,
            pltpu.SemaphoreType.DMA((4,)),
            pltpu.SemaphoreType.DMA((4,)),
        ],
        compiler_params=pltpu.CompilerParams(collective_id=0, has_side_effects=True),
    )(beam_profile, beam_start, beam_steps, layer_heat_coefficients, wafer_state)


def solution(mesh):
    in_specs = (P("scan", "cross", None), P(), P(), P(), P())
    out_specs = P("scan", "cross", None)
    return jax.shard_map(shards, mesh=mesh, in_specs=in_specs, out_specs=out_specs, check_vma=False)
```

profile of v0, /device:TPU:24, one launch (start us, length us, event | category | flops | bytes accessed | tf_op | source)
XLA Modules:
  0.0 65.1 jit_solution(4105492713311165067)
XLA Ops:
  0.0 63.3 %shard_map.55 = f32[16,16,384]{2,1,0:T(8,128)} custom-call(f32[512]{0:T(512)} %profile_ref.1, s32[4]{0:T(128)} %start_ref.1, s32[4]{0:T(128)} %steps_ref.1, f32[256]{0:T(256)} %coef_ref.1, f32[16,16,384]{2,1,0:T(8,128)} %x_ref.1), custom_call_target="tpu_custom_call" | custom-call | tf_op jit(solution)/shard_map/pallas_call | solution.py:360
  63.3 1.8 %copy.7 = f32[16,16,384]{2,1,0:T(8,128)} copy(f32[16,16,384]{2,1,0:T(8,128)} %shard_map.55) | data formatting | bytes 786432
where the time goes:
time: 65.3 us; the launch traced here: 65.1 us
  Pallas kernels  63.3 us (97%)
  local copies, waits for them, and re-layouts  1.77 us (3%)
    pallas_call x1, Pallas kernels, shards(): pl.pallas_call(kernel, out_shape=jax.ShapeDtypeStruct(wafer_state.shape,...  63.3 us
    unnamed x1, local copies, waits for them, and re-layouts  1.77 us

commit v1 on v0

v1 whole, which is shorter than its diff:
```python
import jax
import jax.numpy as jnp
from jax import lax
from jax.experimental import pallas as pl
from jax.experimental.pallas import tpu as pltpu
from jax.sharding import PartitionSpec as P

STEPS = 4
SUBSTEPS = 2
LEVELS = STEPS * SUBSTEPS
HALO = LEVELS
PAD = 8
PADP = 3
LOG2E = 1.4426950408889634
MESH = pl.DeviceIdType.MESH

heat_power = 0.5
absorb_depth = 6.0
barrier_energy = 3.0
frequency_multiplier = 0.6
proton_mobility = 0.15


def lane_roll(v, shift):
    return pltpu.roll(v, shift % v.shape[1], axis=1)


def kernel(
    profile_ref, start_ref, steps_ref, coef_ref, x_ref, o_ref,
    land, stage, ub0, ub1, kb0, kb1, ab0, ab1, db0, db1, pb, spot, pa, send_sems, recv_sems, own_sem, out_sems, got_sems,
):
    s = lax.axis_index("scan")
    c = lax.axis_index("cross")
    n_scan = lax.axis_size("scan")
    n_cross = lax.axis_size("cross")
    rows = x_ref.shape[0]
    cols = x_ref.shape[1]
    total_x = rows * n_scan
    target = (lax.rem(s + n_scan - STEPS, n_scan), c)
    source = (lax.rem(s + STEPS, n_scan), c)
    f32 = jnp.float32
    ub, kb, ab, db = (ub0, ub1), (kb0, kb1), (ab0, ab1), (db0, db1)

    barrier = pltpu.get_barrier_semaphore()
    sides = [(ds, dc) for dc in (-1, 1, 0) for ds in (0, -1, 1) if (ds, dc) != (0, 0)]

    def peer(ds, dc):
        return (lax.rem(s + ds + n_scan, n_scan), c + dc)

    def exists(dc):
        if dc < 0:
            return c > 0
        if dc > 0:
            return c < n_cross - 1
        return None

    def guarded(dc, fn):
        cond = exists(dc)
        if cond is None:
            fn()
        else:
            pl.when(cond)(fn)

    for ds, dc in sides:
        def greet(ds=ds, dc=dc):
            pl.semaphore_signal(barrier, 1, device_id=peer(ds, dc), device_id_type=MESH)
        guarded(dc, greet)
    pl.semaphore_signal(barrier, 1, device_id=target, device_id_type=MESH)

    own = pltpu.make_async_copy(
        x_ref, land.at[pl.ds(HALO, rows), pl.ds(HALO, cols), :], own_sem
    )
    own.start()

    edges = jnp.where(c > 0, 1, 0) + jnp.where(c < n_cross - 1, 1, 0)
    pl.semaphore_wait(barrier, 3 + 3 * edges)

    def span(d, length, sending):
        if d == 0:
            return pl.ds(0 if sending else HALO, length)
        if d > 0:
            return pl.ds(length - HALO if sending else 0, HALO)
        return pl.ds(0 if sending else HALO + length, HALO)

    copies = {}
    for k, (ds, dc) in enumerate(sides):
        copies[(ds, dc)] = pltpu.make_async_remote_copy(
            src_ref=x_ref.at[span(ds, rows, True), span(dc, cols, True), :],
            dst_ref=land.at[span(ds, rows, False), span(dc, cols, False), :],
            send_sem=send_sems.at[k],
            recv_sem=recv_sems.at[k],
            device_id=peer(ds, dc),
            device_id_type=MESH,
        )
    for ds, dc in sides:
        if ds == 0:
            guarded(dc, copies[(ds, dc)].start)

    lane = lax.broadcasted_iota(jnp.int32, (8, 128), 1)
    sub = lax.broadcasted_iota(jnp.int32, (8, 128), 0)
    low = lane < 64
    last_lane = lane == 127
    first_lane = lane == 0
    half_coef = [
        jnp.broadcast_to((0.5 * coef_ref[pl.ds(128 * h, 128)])[None, :], (8, 128)) for h in range(2)
    ]
    floor_coef = half_coef[1]

    for t in range(1, LEVELS + 1):
        f = (t - 1) // SUBSTEPS
        n = (t - 1) % SUBSTEPS
        center = (start_ref[f] + n * steps_ref[f]).astype(f32)
        for g in range(4):
            at = sub + (8 * g - HALO) + (s * rows - rows * f + 2 * total_x)
            where_x = lax.rem(at, jnp.int32(total_x)).astype(f32)
            ratio = (where_x - center) * (1.0 / float(rows // 2))
            spot[pl.ds((t - 1) * 32 + 8 * g, 8), :] = jnp.exp(-ratio * ratio)

    z0 = lane.astype(f32)
    absorb = [
        jnp.where(z0 + (128.0 * h) >= 64.0, jnp.exp(-(z0 + (128.0 * h - 64.0)) / absorb_depth), 0.0)
        for h in range(2)
    ]
    for j in range(4):
        shine = jnp.zeros((8, 128), f32)
        for i in range(8):
            place = c * cols - HALO + 8 * j + i
            place = jnp.clip(place, 0, n_cross * cols - 1)
            shine = jnp.where(sub == i, profile_ref[place], shine)
        for h in range(2):
            pa[h, pl.ds(8 * j, 8), :] = (0.5 * heat_power) * shine * absorb[h]

    left_f = jnp.where(c > 0, 1.0, 0.0).astype(f32)
    right_f = jnp.where(c < n_cross - 1, 1.0, 0.0).astype(f32)
    edge_f = [left_f, None, None, right_f]
    edge_a = [jnp.where(low, left_f, 1.0), jnp.where(low, 1.0, right_f)]

    def col(j, dy=0):
        return pl.ds(PAD + 8 * j + dy, 8)

    def put_cell(b, X, j, u):
        for h in range(2):
            ub[b][h, X, col(j), :] = u[h]
            kb[b][h, X, col(j), :] = half_coef[h] * (1.0 / (1.0 + u[h] * u[h]))

    def put_acid(b, X, g, acid, u_low, u_high):
        u = jnp.where(low, u_low, lane_roll(u_high, 64))
        sq = u * u
        d = (0.5 * proton_mobility * sq) * (1.0 / (0.25 + sq))
        ghost = pl.ds(PAD + 16, 8) if g == 0 else pl.ds(0, 8)
        ab[b][X, col(g), :] = acid
        ab[b][X, ghost, :] = lane_roll(acid, 64)
        db[b][X, col(g), :] = d
        db[b][X, ghost, :] = lane_roll(d, 64)

    def init_rows(first, count):
        def body(i, carry):
            X = first + HALO + i
            u0 = []
            for j in range(4):
                u = [0.5 * land[X, pl.ds(8 * j, 8), pl.ds(128 * h, 128)] for h in range(2)]
                put_cell(0, X, j, u)
                u0.append(u[0])
            for g in range(2):
                acid = jnp.where(
                    low,
                    land[X, pl.ds(8 * g, 8), pl.ds(256, 128)],
                    lane_roll(land[X, pl.ds(8 * g + 16, 8), pl.ds(256, 128)], 64),
                )
                put_acid(0, X, g, acid, u0[g], u0[g + 2])
            return carry

        lax.fori_loop(0, count, body, 0)

    inner_a = jnp.where(lax.rem(lane, 64) < 63, 1.0, 0.0).astype(f32)

    def block(t, r0, a, b, n):
        X0 = r0 + HALO
        beams = [
            jnp.broadcast_to(spot[pl.ds((t - 1) * 32 + X0 + i, 1), :], (8, 128)) for i in range(n)
        ]

        def side(vals, facs, i, load_v, load_f):
            cur, fac = vals[i], facs[i]
            flux_up = (fac + load_f(i, 1)) * (load_v(i, 1) - cur)
            flux_dn = (fac + load_f(i, -1)) * (cur - load_v(i, -1))
            return flux_up - flux_dn

        def along(vals, facs):
            flux = [(facs[i] + facs[i + 1]) * (vals[i + 1] - vals[i]) for i in range(-1, n)]
            return [flux[i + 1] - flux[i] for i in range(n)]

        fresh = {}
        for g in range(2):
            for j in (g, g + 2):
                U = [
                    {i: ub[a][h, X0 + i, col(j), :] for i in range(-1, n + 1)} for h in range(2)
                ]
                K = [
                    {i: kb[a][h, X0 + i, col(j), :] for i in range(-1, n + 1)} for h in range(2)
                ]
                xn = [along(U[h], K[h]) for h in range(2)]
                for i in range(n):
                    ur = [lane_roll(U[h][i], -1) for h in range(2)]
                    kr = [lane_roll(K[h][i], -1) for h in range(2)]
                    un = [jnp.where(last_lane, ur[1], ur[0]), jnp.where(last_lane, 0.0, ur[1])]
                    kn = [jnp.where(last_lane, kr[1], kr[0]), jnp.where(last_lane, floor_coef, kr[1])]
                    fz = [(K[h][i] + kn[h]) * (un[h] - U[h][i]) for h in range(2)]
                    fr = [lane_roll(fz[h], 1) for h in range(2)]
                    fp = [jnp.where(first_lane, 0.0, fr[0]), jnp.where(first_lane, fr[0], fr[1])]
                    out = []
                    for h in range(2):
                        yn = side(
                            U[h], K[h], i,
                            lambda i, dy, h=h: ub[a][h, X0 + i, col(j, dy), :],
                            lambda i, dy, h=h: kb[a][h, X0 + i, col(j, dy), :],
                        )
                        value = U[h][i] + ((xn[h][i] + yn) + (fz[h] - fp[h]))
                        value = value + beams[i] * pa[h, pl.ds(8 * j, 8), :]
                        if edge_f[j] is not None:
                            value = value * edge_f[j]
                        out.append(value)
                    put_cell(b, X0 + i, j, out)
                    fresh[j, i] = out[0]
            A = {i: ab[a][X0 + i, col(g), :] for i in range(-1, n + 1)}
            D = {i: db[a][X0 + i, col(g), :] for i in range(-1, n + 1)}
            xa = along(A, D)
            for i in range(n):
                fz = ((D[i] + lane_roll(D[i], -1)) * (lane_roll(A[i], -1) - A[i])) * inner_a
                ya = side(
                    A, D, i,
                    lambda i, dy: ab[a][X0 + i, col(g, dy), :],
                    lambda i, dy: db[a][X0 + i, col(g, dy), :],
                )
                value = A[i] + ((xa[i] + ya) + (fz - lane_roll(fz, 1)))
                value = value * edge_a[g]
                put_acid(b, X0 + i, g, value, fresh[g, i], fresh[g + 2, i])

        @pl.when(jnp.logical_and(r0 > -n, r0 < rows))
        def _():
            for i in range(n):
                r = r0 + i + PADP
                tp = jnp.where(
                    low, ub[a][0, X0 + i, col(1), :], lane_roll(ub[a][0, X0 + i, col(2), :], 64)
                )
                ap = jnp.where(low, ab[a][X0 + i, col(1), :], ab[a][X0 + i, col(0), :])
                rate = jnp.exp2((-0.5 * barrier_energy * LOG2E) * (1.0 / (0.5 + tp)))
                pb[r] = pb[r] * (1.0 - (frequency_multiplier * ap) * rate)

        for i in range(n):
            r = r0 + i
            owner = lax.rem(s + lax.div(r + rows, rows) - 1 + n_scan, n_scan)

            if b == 1:
                continue

            @pl.when(owner == lax.div(t, 2) - 1)
            def _(i=i):
                zero = jnp.zeros((8, 128), f32)
                for j in range(4):
                    for h in range(2):
                        ub[b][h, X0 + i, col(j), :] = zero
                        kb[b][h, X0 + i, col(j), :] = half_coef[h]
                for g in range(4):
                    db[b][X0 + i, pl.ds(8 * g, 8), :] = zero

    def levels_in_pairs(level, levels):
        def two(n, carry):
            level(2 * n + 1, 0, 1)
            if levels % 2 == 0:
                level(2 * n + 2, 1, 0)
            else:
                pl.when(2 * n + 2 <= levels)(lambda: level(2 * n + 2, 1, 0))
            return carry

        lax.fori_loop(0, (levels + 1) // 2, two, 0)

    def middle():
        def level(t, a, b):
            def four(i, carry):
                block(t, t + 4 * i, a, b, 4)
                return carry

            lax.fori_loop(0, lax.div(rows - 2 * t, 4), four, 0)
            if b == 1:
                block(t, rows - 2 - t, a, b, 2)

        levels_in_pairs(level, LEVELS - 1)

    def flank(first, slope):
        levels_in_pairs(lambda t, a, b: block(t, first + slope * t, a, b, 4), LEVELS)

    def unpack(first, count):
        def body(i, carry):
            r = first + i
            X = r + HALO
            packed = pb[r + PADP]
            for j in (1, 2):
                for h in range(2):
                    stage[r, pl.ds(8 * j - 8, 8), pl.ds(128 * h, 128)] = 2.0 * ub[0][h, X, col(j), :]
            stage[r, pl.ds(0, 8), pl.ds(256, 128)] = jnp.where(
                low, ab[0][X, col(1), :], lane_roll(packed, 64)
            )
            stage[r, pl.ds(8, 8), pl.ds(256, 128)] = jnp.where(
                low, lane_roll(ab[0][X, col(0), :], 64), packed
            )
            return carry

        lax.fori_loop(0, count, body, 0)

    own.wait()

    def pack(i, carry):
        X = HALO + i
        pb[i + PADP] = jnp.where(
            low,
            lane_roll(land[X, pl.ds(8, 8), pl.ds(256, 128)], 64),
            land[X, pl.ds(16, 8), pl.ds(256, 128)],
        )
        return carry

    lax.fori_loop(0, rows, pack, 0)
    for r in range(PADP):
        pb[r] = jnp.zeros((8, 128), f32)
        pb[rows + PADP + r] = jnp.zeros((8, 128), f32)

    def clear(j):
        def body(X, carry):
            for h in range(3):
                land[X, pl.ds(8 * j, 8), pl.ds(128 * h, 128)] = jnp.zeros((8, 128), f32)
            return carry

        lax.fori_loop(0, rows + 2 * HALO, body, 0)

    pl.when(c == 0)(lambda: clear(0))
    pl.when(c == n_cross - 1)(lambda: clear(3))

    def margins(X, carry):
        for b in range(2):
            for h in range(2):
                for j in (-1, 4):
                    ub[b][h, X, col(j), :] = jnp.zeros((8, 128), f32)
                    kb[b][h, X, col(j), :] = jnp.zeros((8, 128), f32)
        return carry

    lax.fori_loop(0, rows + 2 * HALO, margins, 0)

    def arrive(ds):
        for dc in (-1, 0, 1):
            if (ds, dc) != (0, 0):
                k = sides.index((-ds, -dc))
                wait = pltpu.make_async_remote_copy(
                    src_ref=x_ref.at[span(-ds, rows, True), span(-dc, cols, True), :],
                    dst_ref=land.at[span(-ds, rows, False), span(-dc, cols, False), :],
                    send_sem=send_sems.at[k],
                    recv_sem=recv_sems.at[k],
                    device_id=peer(ds, dc),
                    device_id_type=MESH,
                )
                guarded(dc, wait.wait_recv)

    def out_copy(part):
        return pltpu.make_async_remote_copy(
            src_ref=stage.at[pl.ds(4 * part, 4)],
            dst_ref=o_ref.at[pl.ds(4 * part, 4)],
            send_sem=out_sems.at[part],
            recv_sem=got_sems.at[part],
            device_id=target,
            device_id_type=MESH,
        )

    def finish(part, first, slope):
        init_rows(first, 4)
        flank(first, slope)
        unpack(4 * part, 4)
        out_copy(part).start()

    arrive(0)
    for ds, dc in sides:
        if ds != 0:
            guarded(dc, copies[(ds, dc)].start)
    init_rows(0, rows)
    middle()
    arrive(-1)

    def before(i, carry):
        finish(1 - i, -4 - 4 * i, 1)
        return carry

    def after(i, carry):
        finish(2 + i, rows + 4 * i, -1)
        return carry

    lax.fori_loop(0, 2, before, 0)
    arrive(1)
    lax.fori_loop(0, 2, after, 0)
    for part in range(4):
        out_copy(part).wait()
    for ds, dc in sides:
        guarded(dc, copies[(ds, dc)].wait_send)


def shards(wafer_state, layer_heat_coefficients, beam_profile, beam_start, beam_steps):
    smem = pl.BlockSpec(memory_space=pltpu.SMEM)
    f32 = jnp.float32
    rows, cols, chans = wafer_state.shape
    X = rows + 2 * HALO
    Y = cols + 2 * HALO
    return pl.pallas_call(
        kernel,
        out_shape=jax.ShapeDtypeStruct(wafer_state.shape, f32),
        in_specs=[smem, smem, smem, pl.BlockSpec(memory_space=pltpu.VMEM), pl.BlockSpec(memory_space=pl.ANY)],
        out_specs=pl.BlockSpec(memory_space=pl.ANY),
        scratch_shapes=[
            pltpu.VMEM((X, Y, chans), f32),
            pltpu.VMEM((rows, cols, chans), f32),
            pltpu.VMEM((2, X, Y + 2 * PAD, 128), f32),
            pltpu.VMEM((2, X, Y + 2 * PAD, 128), f32),
            pltpu.VMEM((2, X, Y + 2 * PAD, 128), f32),
            pltpu.VMEM((2, X, Y + 2 * PAD, 128), f32),
            pltpu.VMEM((X, 16 + 2 * PAD, 128), f32),
            pltpu.VMEM((X, 16 + 2 * PAD, 128), f32),
            pltpu.VMEM((X, 16 + 2 * PAD, 128), f32),
            pltpu.VMEM((X, 16 + 2 * PAD, 128), f32),
            pltpu.VMEM((rows + 2 * PADP, 8, 128), f32),
            pltpu.VMEM((LEVELS * X, 128), f32),
            pltpu.VMEM((2, Y, 128), f32),
            pltpu.SemaphoreType.DMA((8,)),
            pltpu.SemaphoreType.DMA((8,)),
            pltpu.SemaphoreType.DMA,
            pltpu.SemaphoreType.DMA((4,)),
            pltpu.SemaphoreType.DMA((4,)),
        ],
        compiler_params=pltpu.CompilerParams(collective_id=0, has_side_effects=True),
    )(beam_profile, beam_start, beam_steps, layer_heat_coefficients, wafer_state)


def solution(mesh):
    in_specs = (P("scan", "cross", None), P(), P(), P(), P())
    out_specs = P("scan", "cross", None)
    return jax.shard_map(shards, mesh=mesh, in_specs=in_specs, out_specs=out_specs, check_vma=False)
```

time: 65.3 us -> 48.3 us (0.74)
  Pallas kernels: 63.3 us -> 46.4 us
    pallas_call x1, Pallas kernels: 63.3 us -> 46.4 us  [shards(): pl.pallas_call(kernel, out_shape=jax.ShapeDtypeStruct(wafer_state.shape,...]
where the time goes in v1:
time: 48.3 us; the launch traced here: 48.2 us
  Pallas kernels  46.4 us (96%)
  local copies, waits for them, and re-layouts  1.77 us (4%)
    pallas_call x1, Pallas kernels, shards(): pl.pallas_call(kernel, out_shape=jax.ShapeDtypeStruct(wafer_state.shape,...  46.4 us
    unnamed x1, local copies, waits for them, and re-layouts  1.77 us

profile of v1, /device:TPU:24, one launch (start us, length us, event | category | flops | bytes accessed | tf_op | source)
XLA Modules:
  0.0 48.2 jit_solution(9695989526349841337)
XLA Ops:
  0.0 46.4 %shard_map.55 = f32[16,16,384]{2,1,0:T(8,128)} custom-call(f32[512]{0:T(512)} %profile_ref.1, s32[4]{0:T(128)} %start_ref.1, s32[4]{0:T(128)} %steps_ref.1, f32[256]{0:T(256)} %coef_ref.1, f32[16,16,384]{2,1,0:T(8,128)} %x_ref.1), custom_call_target="tpu_custom_call" | custom-call | tf_op jit(solution)/shard_map/pallas_call | solution.py:409
  46.4 1.8 %copy.7 = f32[16,16,384]{2,1,0:T(8,128)} copy(f32[16,16,384]{2,1,0:T(8,128)} %shard_map.55) | data formatting | bytes 786432

commit v2 on v1

--- a/solution.py
+++ b/solution.py
@@ -9,6 +9,7 @@
 SUBSTEPS = 2
 LEVELS = STEPS * SUBSTEPS
 HALO = LEVELS
+REACH = LEVELS // 2
 PAD = 8
 PADP = 3
 LOG2E = 1.4426950408889634
@@ -27,7 +28,8 @@
 
 def kernel(
     profile_ref, start_ref, steps_ref, coef_ref, x_ref, o_ref,
-    land, stage, ub0, ub1, kb0, kb1, ab0, ab1, db0, db1, pb, spot, pa, send_sems, recv_sems, own_sem, out_sems, got_sems,
+    land, stage, send_u, send_a, land_u, land_a, ub0, ub1, kb0, kb1, ab0, ab1, db0, db1, pb, spot, pa, send_sems, recv_sems, own_sem, out_sems, got_sems,
+    mid_send_sems, mid_recv_sems,
 ):
     s = lax.axis_index("scan")
     c = lax.axis_index("cross")
@@ -68,25 +70,25 @@
     pl.semaphore_signal(barrier, 1, device_id=target, device_id_type=MESH)
 
     own = pltpu.make_async_copy(
-        x_ref, land.at[pl.ds(HALO, rows), pl.ds(HALO, cols), :], own_sem
+        x_ref, land.at[pl.ds(REACH, rows), pl.ds(HALO, cols), :], own_sem
     )
     own.start()
 
     edges = jnp.where(c > 0, 1, 0) + jnp.where(c < n_cross - 1, 1, 0)
     pl.semaphore_wait(barrier, 3 + 3 * edges)
 
-    def span(d, length, sending):
+    def span(d, length, sending, halo):
         if d == 0:
-            return pl.ds(0 if sending else HALO, length)
+            return pl.ds(0 if sending else halo, length)
         if d > 0:
-            return pl.ds(length - HALO if sending else 0, HALO)
-        return pl.ds(0 if sending else HALO + length, HALO)
+            return pl.ds(length - halo if sending else 0, halo)
+        return pl.ds(0 if sending else halo + length, halo)
 
     copies = {}
     for k, (ds, dc) in enumerate(sides):
         copies[(ds, dc)] = pltpu.make_async_remote_copy(
-            src_ref=x_ref.at[span(ds, rows, True), span(dc, cols, True), :],
-            dst_ref=land.at[span(ds, rows, False), span(dc, cols, False), :],
+            src_ref=x_ref.at[span(ds, rows, True, REACH), span(dc, cols, True, HALO), :],
+            dst_ref=land.at[span(ds, rows, False, REACH), span(dc, cols, False, HALO), :],
             send_sem=send_sems.at[k],
             recv_sem=recv_sems.at[k],
             device_id=peer(ds, dc),
@@ -110,11 +112,11 @@
         f = (t - 1) // SUBSTEPS
         n = (t - 1) % SUBSTEPS
         center = (start_ref[f] + n * steps_ref[f]).astype(f32)
-        for g in range(4):
-            at = sub + (8 * g - HALO) + (s * rows - rows * f + 2 * total_x)
+        for g in range(3):
+            at = sub + (8 * g - REACH) + (s * rows - rows * f + 2 * total_x)
             where_x = lax.rem(at, jnp.int32(total_x)).astype(f32)
             ratio = (where_x - center) * (1.0 / float(rows // 2))
-            spot[pl.ds((t - 1) * 32 + 8 * g, 8), :] = jnp.exp(-ratio * ratio)
+            spot[pl.ds((t - 1) * 24 + 8 * g, 8), :] = jnp.exp(-ratio * ratio)
 
     z0 = lane.astype(f32)
     absorb = [
@@ -155,7 +157,7 @@
 
     def init_rows(first, count):
         def body(i, carry):
-            X = first + HALO + i
+            X = first + REACH + i
             u0 = []
             for j in range(4):
                 u = [0.5 * land[X, pl.ds(8 * j, 8), pl.ds(128 * h, 128)] for h in range(2)]
@@ -175,9 +177,9 @@
     inner_a = jnp.where(lax.rem(lane, 64) < 63, 1.0, 0.0).astype(f32)
 
     def block(t, r0, a, b, n):
-        X0 = r0 + HALO
+        X0 = r0 + REACH
         beams = [
-            jnp.broadcast_to(spot[pl.ds((t - 1) * 32 + X0 + i, 1), :], (8, 128)) for i in range(n)
+            jnp.broadcast_to(spot[pl.ds((t - 1) * 24 + X0 + i, 1), :], (8, 128)) for i in range(n)
         ]
 
         def side(vals, facs, i, load_v, load_f):
@@ -264,36 +266,33 @@
                 for g in range(4):
                     db[b][X0 + i, pl.ds(8 * g, 8), :] = zero
 
-    def levels_in_pairs(level, levels):
-        def two(n, carry):
-            level(2 * n + 1, 0, 1)
-            if levels % 2 == 0:
-                level(2 * n + 2, 1, 0)
-            else:
-                pl.when(2 * n + 2 <= levels)(lambda: level(2 * n + 2, 1, 0))
+    def levels_in_pairs(level, base):
+        def two(m, carry):
+            level(2 * m + 1, base + 2 * m + 1, 0, 1)
+            level(2 * m + 2, base + 2 * m + 2, 1, 0)
             return carry
 
-        lax.fori_loop(0, (levels + 1) // 2, two, 0)
-
-    def middle():
-        def level(t, a, b):
+        lax.fori_loop(0, REACH // 2, two, 0)
+
+    def middle(base):
+        def level(k, t, a, b):
             def four(i, carry):
-                block(t, t + 4 * i, a, b, 4)
+                block(t, k + 4 * i, a, b, 4)
                 return carry
 
-            lax.fori_loop(0, lax.div(rows - 2 * t, 4), four, 0)
+            lax.fori_loop(0, lax.div(rows - 2 * k, 4), four, 0)
             if b == 1:
-                block(t, rows - 2 - t, a, b, 2)
-
-        levels_in_pairs(level, LEVELS - 1)
-
-    def flank(first, slope):
-        levels_in_pairs(lambda t, a, b: block(t, first + slope * t, a, b, 4), LEVELS)
+                block(t, rows - 2 - k, a, b, 2)
+
+        levels_in_pairs(level, base)
+
+    def flank(base, first, slope):
+        levels_in_pairs(lambda k, t, a, b: block(t, first + slope * k, a, b, 4), base)
 
     def unpack(first, count):
         def body(i, carry):
             r = first + i
-            X = r + HALO
+            X = r + REACH
             packed = pb[r + PADP]
             for j in (1, 2):
                 for h in range(2):
@@ -311,7 +310,7 @@
     own.wait()
 
     def pack(i, carry):
-        X = HALO + i
+        X = REACH + i
         pb[i + PADP] = jnp.where(
             low,
             lane_roll(land[X, pl.ds(8, 8), pl.ds(256, 128)], 64),
@@ -330,7 +329,7 @@
                 land[X, pl.ds(8 * j, 8), pl.ds(128 * h, 128)] = jnp.zeros((8, 128), f32)
             return carry
 
-        lax.fori_loop(0, rows + 2 * HALO, body, 0)
+        lax.fori_loop(0, rows + 2 * REACH, body, 0)
 
     pl.when(c == 0)(lambda: clear(0))
     pl.when(c == n_cross - 1)(lambda: clear(3))
@@ -343,15 +342,15 @@
                     kb[b][h, X, col(j), :] = jnp.zeros((8, 128), f32)
         return carry
 
-    lax.fori_loop(0, rows + 2 * HALO, margins, 0)
+    lax.fori_loop(0, rows + 2 * REACH, margins, 0)
 
     def arrive(ds):
         for dc in (-1, 0, 1):
             if (ds, dc) != (0, 0):
                 k = sides.index((-ds, -dc))
                 wait = pltpu.make_async_remote_copy(
-                    src_ref=x_ref.at[span(-ds, rows, True), span(-dc, cols, True), :],
-                    dst_ref=land.at[span(-ds, rows, False), span(-dc, cols, False), :],
+                    src_ref=x_ref.at[span(-ds, rows, True, REACH), span(-dc, cols, True, HALO), :],
+                    dst_ref=land.at[span(-ds, rows, False, REACH), span(-dc, cols, False, HALO), :],
                     send_sem=send_sems.at[k],
                     recv_sem=recv_sems.at[k],
                     device_id=peer(ds, dc),
@@ -375,27 +374,80 @@
         unpack(4 * part, 4)
         out_copy(part).start()
 
+    def mid_copies(side):
+        to = peer(2 * side - 1, 0)
+        return [
+            pltpu.make_async_remote_copy(
+                src_ref=src.at[side],
+                dst_ref=dst.at[1 - side],
+                send_sem=mid_send_sems.at[2 * side + n],
+                recv_sem=mid_recv_sems.at[2 * side + n],
+                device_id=to,
+                device_id_type=MESH,
+            )
+            for n, (src, dst) in enumerate(((send_u, land_u), (send_a, land_a)))
+        ]
+
+    def give(side):
+        for i in range(REACH):
+            X = REACH + i + side * (rows - REACH)
+            for j in range(4):
+                for h in range(2):
+                    send_u[side, h, i, pl.ds(8 * j, 8), :] = ub[0][h, X, col(j), :]
+            for g in range(2):
+                send_a[side, i, pl.ds(8 * g, 8), :] = ab[0][X, col(g), :]
+        for copy in mid_copies(side):
+            copy.start()
+
+    def take(side):
+        for copy in mid_copies(1 - side):
+            copy.wait_recv()
+
+        def body(i, carry):
+            X = i + side * (rows + REACH)
+            u0 = []
+            for j in range(4):
+                u = [land_u[side, h, i, pl.ds(8 * j, 8), :] for h in range(2)]
+                put_cell(0, X, j, u)
+                u0.append(u[0])
+            for g in range(2):
+                put_acid(0, X, g, land_a[side, i, pl.ds(8 * g, 8), :], u0[g], u0[g + 2])
+            return carry
+
+        lax.fori_loop(0, REACH, body, 0)
+
+    def finish(part):
+        unpack(4 * part, 4)
+        out_copy(part).start()
+
     arrive(0)
     for ds, dc in sides:
         if ds != 0:
             guarded(dc, copies[(ds, dc)].start)
     init_rows(0, rows)
-    middle()
+    middle(0)
     arrive(-1)
-
-    def before(i, carry):
-        finish(1 - i, -4 - 4 * i, 1)
-        return carry
-
-    def after(i, carry):
-        finish(2 + i, rows + 4 * i, -1)
-        return carry
-
-    lax.fori_loop(0, 2, before, 0)
+    init_rows(-4, 4)
+    flank(0, -4, 1)
+    give(0)
     arrive(1)
-    lax.fori_loop(0, 2, after, 0)
+    init_rows(rows, 4)
+    flank(0, rows, -1)
+    give(1)
+    middle(REACH)
+    finish(1)
+    finish(2)
+    take(0)
+    flank(REACH, -4, 1)
+    finish(0)
+    take(1)
+    flank(REACH, rows, -1)
+    finish(3)
     for part in range(4):
         out_copy(part).wait()
+    for side in range(2):
+        for copy in mid_copies(side):
+            copy.wait_send()
     for ds, dc in sides:
         guarded(dc, copies[(ds, dc)].wait_send)
 
@@ -404,7 +456,7 @@
     smem = pl.BlockSpec(memory_space=pltpu.SMEM)
     f32 = jnp.float32
     rows, cols, chans = wafer_state.shape
-    X = rows + 2 * HALO
+    X = rows + 2 * REACH
     Y = cols + 2 * HALO
     return pl.pallas_call(
         kernel,
@@ -414,6 +466,10 @@
         scratch_shapes=[
             pltpu.VMEM((X, Y, chans), f32),
             pltpu.VMEM((rows, cols, chans), f32),
+            pltpu.VMEM((2, 2, REACH, Y, 128), f32),
+            pltpu.VMEM((2, REACH, 16, 128), f32),
+            pltpu.VMEM((2, 2, REACH, Y, 128), f32),
+            pltpu.VMEM((2, REACH, 16, 128), f32),
             pltpu.VMEM((2, X, Y + 2 * PAD, 128), f32),
             pltpu.VMEM((2, X, Y + 2 * PAD, 128), f32),
             pltpu.VMEM((2, X, Y + 2 * PAD, 128), f32),
@@ -423,13 +479,15 @@
             pltpu.VMEM((X, 16 + 2 * PAD, 128), f32),
             pltpu.VMEM((X, 16 + 2 * PAD, 128), f32),
             pltpu.VMEM((rows + 2 * PADP, 8, 128), f32),
-            pltpu.VMEM((LEVELS * X, 128), f32),
+            pltpu.VMEM((LEVELS * 24, 128), f32),
             pltpu.VMEM((2, Y, 128), f32),
             pltpu.SemaphoreType.DMA((8,)),
             pltpu.SemaphoreType.DMA((8,)),
             pltpu.SemaphoreType.DMA,
             pltpu.SemaphoreType.DMA((4,)),
             pltpu.SemaphoreType.DMA((4,)),
+            pltpu.SemaphoreType.DMA((4,)),
+            pltpu.SemaphoreType.DMA((4,)),
         ],
         compiler_params=pltpu.CompilerParams(collective_id=0, has_side_effects=True),
     )(beam_profile, beam_start, beam_steps, layer_heat_coefficients, wafer_state)

time: 48.3 us -> 45.9 us (0.950)
  Pallas kernels: 46.4 us -> 43.9 us
    pallas_call x1, Pallas kernels: 46.4 us -> 43.9 us  [shards(): pl.pallas_call(kernel, out_shape=jax.ShapeDtypeStruct(wafer_state.shape,...]
where the time goes in v2:
time: 45.9 us; the launch traced here: 45.7 us
  Pallas kernels  43.9 us (96%)
  local copies, waits for them, and re-layouts  1.77 us (4%)
    pallas_call x1, Pallas kernels, shards(): pl.pallas_call(kernel, out_shape=jax.ShapeDtypeStruct(wafer_state.shape,...  43.9 us
    unnamed x1, local copies, waits for them, and re-layouts  1.77 us

profile of v2, /device:TPU:24, one launch (start us, length us, event | category | flops | bytes accessed | tf_op | source)
XLA Modules:
  0.0 45.7 jit_solution(8255778003779951724)
XLA Ops:
  0.0 43.9 %shard_map.55 = f32[16,16,384]{2,1,0:T(8,128)} custom-call(f32[512]{0:T(512)} %profile_ref.1, s32[4]{0:T(128)} %start_ref.1, s32[4]{0:T(128)} %steps_ref.1, f32[256]{0:T(256)} %coef_ref.1, f32[16,16,384]{2,1,0:T(8,128)} %x_ref.1), custom_call_target="tpu_custom_call" | custom-call | tf_op jit(solution)/shard_map/pallas_call | solution.py:461
  43.9 1.8 %copy.7 = f32[16,16,384]{2,1,0:T(8,128)} copy(f32[16,16,384]{2,1,0:T(8,128)} %shard_map.55) | data formatting | bytes 786432

commit v3 on v2

--- a/solution.py
+++ b/solution.py
@@ -11,7 +11,6 @@
 HALO = LEVELS
 REACH = LEVELS // 2
 PAD = 8
-PADP = 3
 LOG2E = 1.4426950408889634
 MESH = pl.DeviceIdType.MESH
 
@@ -44,7 +43,7 @@
     ub, kb, ab, db = (ub0, ub1), (kb0, kb1), (ab0, ab1), (db0, db1)
 
     barrier = pltpu.get_barrier_semaphore()
-    sides = [(ds, dc) for dc in (-1, 1, 0) for ds in (0, -1, 1) if (ds, dc) != (0, 0)]
+    sides = [(0, -1), (0, 1), (-1, 0), (1, 0)]
 
     def peer(ds, dc):
         return (lax.rem(s + ds + n_scan, n_scan), c + dc)
@@ -74,9 +73,6 @@
     )
     own.start()
 
-    edges = jnp.where(c > 0, 1, 0) + jnp.where(c < n_cross - 1, 1, 0)
-    pl.semaphore_wait(barrier, 3 + 3 * edges)
-
     def span(d, length, sending, halo):
         if d == 0:
             return pl.ds(0 if sending else halo, length)
@@ -84,19 +80,22 @@
             return pl.ds(length - halo if sending else 0, halo)
         return pl.ds(0 if sending else halo + length, halo)
 
-    copies = {}
-    for k, (ds, dc) in enumerate(sides):
-        copies[(ds, dc)] = pltpu.make_async_remote_copy(
-            src_ref=x_ref.at[span(ds, rows, True, REACH), span(dc, cols, True, HALO), :],
-            dst_ref=land.at[span(ds, rows, False, REACH), span(dc, cols, False, HALO), :],
+    def halo_copy(ds, dc):
+        k = sides.index((ds, dc))
+        if ds == 0:
+            source_ref = x_ref.at[:, span(dc, cols, True, HALO), :]
+            landing = land.at[pl.ds(REACH, rows), span(dc, cols, False, HALO), :]
+        else:
+            source_ref = land.at[pl.ds(REACH if ds < 0 else rows, REACH)]
+            landing = land.at[span(ds, rows, False, REACH)]
+        return pltpu.make_async_remote_copy(
+            src_ref=source_ref,
+            dst_ref=landing,
             send_sem=send_sems.at[k],
             recv_sem=recv_sems.at[k],
             device_id=peer(ds, dc),
             device_id_type=MESH,
         )
-    for ds, dc in sides:
-        if ds == 0:
-            guarded(dc, copies[(ds, dc)].start)
 
     lane = lax.broadcasted_iota(jnp.int32, (8, 128), 1)
     sub = lax.broadcasted_iota(jnp.int32, (8, 128), 0)
@@ -156,23 +155,22 @@
         db[b][X, ghost, :] = lane_roll(d, 64)
 
     def init_rows(first, count):
-        def body(i, carry):
-            X = first + REACH + i
-            u0 = []
-            for j in range(4):
-                u = [0.5 * land[X, pl.ds(8 * j, 8), pl.ds(128 * h, 128)] for h in range(2)]
-                put_cell(0, X, j, u)
-                u0.append(u[0])
-            for g in range(2):
-                acid = jnp.where(
-                    low,
-                    land[X, pl.ds(8 * g, 8), pl.ds(256, 128)],
-                    lane_roll(land[X, pl.ds(8 * g + 16, 8), pl.ds(256, 128)], 64),
-                )
-                put_acid(0, X, g, acid, u0[g], u0[g + 2])
+        def body(q, carry):
+            for i in range(4):
+                X = first + REACH + 4 * q + i
+                u0 = []
+                for j in range(4):
+                    u = [0.5 * land[X, pl.ds(8 * j, 8), pl.ds(128 * h, 128)] for h in range(2)]
+                    put_cell(0, X, j, u)
+                    u0.append(u[0])
+                last = [land[X, pl.ds(8 * j, 8), pl.ds(256, 128)] for j in range(4)]
+                for g in range(2):
+                    acid = jnp.where(low, last[g], lane_roll(last[g + 2], 64))
+                    put_acid(0, X, g, acid, u0[g], u0[g + 2])
+                pb[X] = jnp.where(low, lane_roll(last[1], 64), last[2])
             return carry
 
-        lax.fori_loop(0, count, body, 0)
+        lax.fori_loop(0, count // 4, body, 0)
 
     inner_a = jnp.where(lax.rem(lane, 64) < 63, 1.0, 0.0).astype(f32)
 
@@ -241,13 +239,12 @@
         @pl.when(jnp.logical_and(r0 > -n, r0 < rows))
         def _():
             for i in range(n):
-                r = r0 + i + PADP
                 tp = jnp.where(
                     low, ub[a][0, X0 + i, col(1), :], lane_roll(ub[a][0, X0 + i, col(2), :], 64)
                 )
                 ap = jnp.where(low, ab[a][X0 + i, col(1), :], ab[a][X0 + i, col(0), :])
                 rate = jnp.exp2((-0.5 * barrier_energy * LOG2E) * (1.0 / (0.5 + tp)))
-                pb[r] = pb[r] * (1.0 - (frequency_multiplier * ap) * rate)
+                pb[X0 + i] = pb[X0 + i] * (1.0 - (frequency_multiplier * ap) * rate)
 
         for i in range(n):
             r = r0 + i
@@ -290,10 +287,10 @@
         levels_in_pairs(lambda k, t, a, b: block(t, first + slope * k, a, b, 4), base)
 
     def unpack(first, count):
-        def body(i, carry):
+        for i in range(count):
             r = first + i
             X = r + REACH
-            packed = pb[r + PADP]
+            packed = pb[X]
             for j in (1, 2):
                 for h in range(2):
                     stage[r, pl.ds(8 * j - 8, 8), pl.ds(128 * h, 128)] = 2.0 * ub[0][h, X, col(j), :]
@@ -303,33 +300,15 @@
             stage[r, pl.ds(8, 8), pl.ds(256, 128)] = jnp.where(
                 low, lane_roll(ab[0][X, col(0), :], 64), packed
             )
-            return carry
-
-        lax.fori_loop(0, count, body, 0)
-
-    own.wait()
-
-    def pack(i, carry):
-        X = REACH + i
-        pb[i + PADP] = jnp.where(
-            low,
-            lane_roll(land[X, pl.ds(8, 8), pl.ds(256, 128)], 64),
-            land[X, pl.ds(16, 8), pl.ds(256, 128)],
-        )
-        return carry
-
-    lax.fori_loop(0, rows, pack, 0)
-    for r in range(PADP):
-        pb[r] = jnp.zeros((8, 128), f32)
-        pb[rows + PADP + r] = jnp.zeros((8, 128), f32)
 
     def clear(j):
-        def body(X, carry):
+        def body(i, carry):
+            X = REACH + i
             for h in range(3):
                 land[X, pl.ds(8 * j, 8), pl.ds(128 * h, 128)] = jnp.zeros((8, 128), f32)
             return carry
 
-        lax.fori_loop(0, rows + 2 * REACH, body, 0)
+        lax.fori_loop(0, rows, body, 0)
 
     pl.when(c == 0)(lambda: clear(0))
     pl.when(c == n_cross - 1)(lambda: clear(3))
@@ -344,19 +323,13 @@
 
     lax.fori_loop(0, rows + 2 * REACH, margins, 0)
 
-    def arrive(ds):
-        for dc in (-1, 0, 1):
-            if (ds, dc) != (0, 0):
-                k = sides.index((-ds, -dc))
-                wait = pltpu.make_async_remote_copy(
-                    src_ref=x_ref.at[span(-ds, rows, True, REACH), span(-dc, cols, True, HALO), :],
-                    dst_ref=land.at[span(-ds, rows, False, REACH), span(-dc, cols, False, HALO), :],
-                    send_sem=send_sems.at[k],
-                    recv_sem=recv_sems.at[k],
-                    device_id=peer(ds, dc),
-                    device_id_type=MESH,
-                )
-                guarded(dc, wait.wait_recv)
+    def arrive(ds, dc):
+        guarded(dc, halo_copy(-ds, -dc).wait_recv)
+
+    pl.semaphore_wait(barrier, 3 + jnp.where(c > 0, 1, 0) + jnp.where(c < n_cross - 1, 1, 0))
+    for dc in (-1, 1):
+        guarded(dc, halo_copy(0, dc).start)
+    own.wait()
 
     def out_copy(part):
         return pltpu.make_async_remote_copy(
@@ -403,7 +376,7 @@
         for copy in mid_copies(1 - side):
             copy.wait_recv()
 
-        def body(i, carry):
+        for i in range(REACH):
             X = i + side * (rows + REACH)
             u0 = []
             for j in range(4):
@@ -412,26 +385,23 @@
                 u0.append(u[0])
             for g in range(2):
                 put_acid(0, X, g, land_a[side, i, pl.ds(8 * g, 8), :], u0[g], u0[g + 2])
-            return carry
-
-        lax.fori_loop(0, REACH, body, 0)
 
     def finish(part):
         unpack(4 * part, 4)
         out_copy(part).start()
 
-    arrive(0)
-    for ds, dc in sides:
-        if ds != 0:
-            guarded(dc, copies[(ds, dc)].start)
+    for dc in (-1, 1):
+        arrive(0, dc)
+    for ds in (-1, 1):
+        halo_copy(ds, 0).start()
     init_rows(0, rows)
     middle(0)
-    arrive(-1)
-    init_rows(-4, 4)
-    flank(0, -4, 1)
+    arrive(-1, 0)
+    init_rows(-REACH, REACH)
+    flank(0, -REACH, 1)
     give(0)
-    arrive(1)
-    init_rows(rows, 4)
+    arrive(1, 0)
+    init_rows(rows, REACH)
     flank(0, rows, -1)
     give(1)
     middle(REACH)
@@ -449,7 +419,7 @@
         for copy in mid_copies(side):
             copy.wait_send()
     for ds, dc in sides:
-        guarded(dc, copies[(ds, dc)].wait_send)
+        guarded(dc, halo_copy(ds, dc).wait_send)
 
 
 def shards(wafer_state, layer_heat_coefficients, beam_profile, beam_start, beam_steps):
@@ -478,11 +448,11 @@
             pltpu.VMEM((X, 16 + 2 * PAD, 128), f32),
             pltpu.VMEM((X, 16 + 2 * PAD, 128), f32),
             pltpu.VMEM((X, 16 + 2 * PAD, 128), f32),
-            pltpu.VMEM((rows + 2 * PADP, 8, 128), f32),
+            pltpu.VMEM((X, 8, 128), f32),
             pltpu.VMEM((LEVELS * 24, 128), f32),
             pltpu.VMEM((2, Y, 128), f32),
-            pltpu.SemaphoreType.DMA((8,)),
-            pltpu.SemaphoreType.DMA((8,)),
+            pltpu.SemaphoreType.DMA((4,)),
+            pltpu.SemaphoreType.DMA((4,)),
             pltpu.SemaphoreType.DMA,
             pltpu.SemaphoreType.DMA((4,)),
             pltpu.SemaphoreType.DMA((4,)),

time: 45.9 us -> 41.5 us (0.904)
  Pallas kernels: 43.9 us -> 39.6 us
    pallas_call x1, Pallas kernels: 43.9 us -> 39.6 us  [shards(): pl.pallas_call(kernel, out_shape=jax.ShapeDtypeStruct(wafer_state.shape,...]
where the time goes in v3:
time: 41.5 us; the launch traced here: 41.3 us
  Pallas kernels  39.6 us (95%)
  local copies, waits for them, and re-layouts  1.77 us (4%)
    pallas_call x1, Pallas kernels, shards(): pl.pallas_call(kernel, out_shape=jax.ShapeDtypeStruct(wafer_state.shape,...  39.6 us
    unnamed x1, local copies, waits for them, and re-layouts  1.77 us

profile of v3, /device:TPU:24, one launch (start us, length us, event | category | flops | bytes accessed | tf_op | source)
XLA Modules:
  0.0 41.3 jit_solution(6985019636226827152)
XLA Ops:
  0.0 39.6 %shard_map.55 = f32[16,16,384]{2,1,0:T(8,128)} custom-call(f32[512]{0:T(512)} %profile_ref.1, s32[4]{0:T(128)} %start_ref.1, s32[4]{0:T(128)} %steps_ref.1, f32[256]{0:T(256)} %coef_ref.1, f32[16,16,384]{2,1,0:T(8,128)} %x_ref.1), custom_call_target="tpu_custom_call" | custom-call | tf_op jit(solution)/shard_map/pallas_call | solution.py:431
  39.6 1.8 %copy.7 = f32[16,16,384]{2,1,0:T(8,128)} copy(f32[16,16,384]{2,1,0:T(8,128)} %shard_map.55) | data formatting | bytes 786432

commit v4 on v3

--- a/solution.py
+++ b/solution.py
@@ -80,14 +80,20 @@
             return pl.ds(length - halo if sending else 0, halo)
         return pl.ds(0 if sending else halo + length, halo)
 
-    def halo_copy(ds, dc):
-        k = sides.index((ds, dc))
+    def halo_copy(ds, dc, part=0):
         if ds == 0:
+            k = sides.index((ds, dc))
             source_ref = x_ref.at[:, span(dc, cols, True, HALO), :]
             landing = land.at[pl.ds(REACH, rows), span(dc, cols, False, HALO), :]
         else:
-            source_ref = land.at[pl.ds(REACH if ds < 0 else rows, REACH)]
-            landing = land.at[span(ds, rows, False, REACH)]
+            k = (2 if ds < 0 else 5) + part
+            if part == 0:
+                places = pl.ds(HALO, cols)
+                source_ref = x_ref.at[span(ds, rows, True, REACH)]
+            else:
+                places = pl.ds(0 if part == 1 else HALO + cols, HALO)
+                source_ref = land.at[pl.ds(REACH if ds < 0 else rows, REACH), places, :]
+            landing = land.at[span(ds, rows, False, REACH), places, :]
         return pltpu.make_async_remote_copy(
             src_ref=source_ref,
             dst_ref=landing,
@@ -174,7 +180,7 @@
 
     inner_a = jnp.where(lax.rem(lane, 64) < 63, 1.0, 0.0).astype(f32)
 
-    def block(t, r0, a, b, n):
+    def block(t, r0, a, b, n, final=False):
         X0 = r0 + REACH
         beams = [
             jnp.broadcast_to(spot[pl.ds((t - 1) * 24 + X0 + i, 1), :], (8, 128)) for i in range(n)
@@ -192,7 +198,7 @@
 
         fresh = {}
         for g in range(2):
-            for j in (g, g + 2):
+            for j in tuple(j for j in (g, g + 2) if not final or j in (1, 2)):
                 U = [
                     {i: ub[a][h, X0 + i, col(j), :] for i in range(-1, n + 1)} for h in range(2)
                 ]
@@ -220,6 +226,10 @@
                         if edge_f[j] is not None:
                             value = value * edge_f[j]
                         out.append(value)
+                    if final:
+                        for h in range(2):
+                            ub[b][h, X0 + i, col(j), :] = out[h]
+                        continue
                     put_cell(b, X0 + i, j, out)
                     fresh[j, i] = out[0]
             A = {i: ab[a][X0 + i, col(g), :] for i in range(-1, n + 1)}
@@ -234,7 +244,10 @@
                 )
                 value = A[i] + ((xa[i] + ya) + (fz - lane_roll(fz, 1)))
                 value = value * edge_a[g]
-                put_acid(b, X0 + i, g, value, fresh[g, i], fresh[g + 2, i])
+                if final:
+                    ab[b][X0 + i, col(g), :] = value
+                else:
+                    put_acid(b, X0 + i, g, value, fresh[g, i], fresh[g + 2, i])
 
         @pl.when(jnp.logical_and(r0 > -n, r0 < rows))
         def _():
@@ -265,26 +278,28 @@
 
     def levels_in_pairs(level, base):
         def two(m, carry):
-            level(2 * m + 1, base + 2 * m + 1, 0, 1)
-            level(2 * m + 2, base + 2 * m + 2, 1, 0)
+            level(2 * m + 1, base + 2 * m + 1, 0, 1, False)
+            level(2 * m + 2, base + 2 * m + 2, 1, 0, False)
             return carry
 
         lax.fori_loop(0, REACH // 2, two, 0)
 
-    def middle(base):
-        def level(k, t, a, b):
+    def middle(base, count):
+        def level(k, t, a, b, final):
             def four(i, carry):
-                block(t, k + 4 * i, a, b, 4)
+                block(t, k + 4 * i, a, b, 4, final)
                 return carry
 
-            lax.fori_loop(0, lax.div(rows - 2 * k, 4), four, 0)
+            lax.fori_loop(0, lax.div(count - 2 * k, 4), four, 0)
             if b == 1:
-                block(t, rows - 2 - k, a, b, 2)
+                block(t, count - 2 - k, a, b, 2, final)
 
         levels_in_pairs(level, base)
 
     def flank(base, first, slope):
-        levels_in_pairs(lambda k, t, a, b: block(t, first + slope * k, a, b, 4), base)
+        levels_in_pairs(
+            lambda k, t, a, b, final: block(t, first + slope * k, a, b, 4, final), base
+        )
 
     def unpack(first, count):
         for i in range(count):
@@ -324,11 +339,14 @@
     lax.fori_loop(0, rows + 2 * REACH, margins, 0)
 
     def arrive(ds, dc):
-        guarded(dc, halo_copy(-ds, -dc).wait_recv)
+        for part in range(3 if dc == 0 else 1):
+            guarded(dc, halo_copy(-ds, -dc, part).wait_recv)
 
     pl.semaphore_wait(barrier, 3 + jnp.where(c > 0, 1, 0) + jnp.where(c < n_cross - 1, 1, 0))
     for dc in (-1, 1):
         guarded(dc, halo_copy(0, dc).start)
+    for ds in (-1, 1):
+        halo_copy(ds, 0).start()
     own.wait()
 
     def out_copy(part):
@@ -393,9 +411,10 @@
     for dc in (-1, 1):
         arrive(0, dc)
     for ds in (-1, 1):
-        halo_copy(ds, 0).start()
+        for part in (1, 2):
+            halo_copy(ds, 0, part).start()
     init_rows(0, rows)
-    middle(0)
+    middle(0, rows)
     arrive(-1, 0)
     init_rows(-REACH, REACH)
     flank(0, -REACH, 1)
@@ -404,22 +423,27 @@
     init_rows(rows, REACH)
     flank(0, rows, -1)
     give(1)
-    middle(REACH)
+    middle(REACH, rows - 4)
     finish(1)
-    finish(2)
-    take(0)
-    flank(REACH, -4, 1)
-    finish(0)
-    take(1)
-    flank(REACH, rows, -1)
-    finish(3)
+
+    def closing(n, carry):
+        pl.when(n == 1)(lambda: take(1))
+        pl.when(n == 2)(lambda: take(0))
+        first = jnp.where(n == 0, rows - 4, jnp.where(n == 1, rows, -REACH))
+        slope = jnp.where(n == 2, 1, -1)
+        flank(REACH, first, slope)
+        finish(jnp.where(n == 0, 2, jnp.where(n == 1, 3, 0)))
+        return carry
+
+    lax.fori_loop(0, 3, closing, 0)
     for part in range(4):
         out_copy(part).wait()
     for side in range(2):
         for copy in mid_copies(side):
             copy.wait_send()
     for ds, dc in sides:
-        guarded(dc, halo_copy(ds, dc).wait_send)
+        for part in range(3 if dc == 0 else 1):
+            guarded(dc, halo_copy(ds, dc, part).wait_send)
 
 
 def shards(wafer_state, layer_heat_coefficients, beam_profile, beam_start, beam_steps):
@@ -451,8 +475,8 @@
             pltpu.VMEM((X, 8, 128), f32),
             pltpu.VMEM((LEVELS * 24, 128), f32),
             pltpu.VMEM((2, Y, 128), f32),
-            pltpu.SemaphoreType.DMA((4,)),
-            pltpu.SemaphoreType.DMA((4,)),
+            pltpu.SemaphoreType.DMA((8,)),
+            pltpu.SemaphoreType.DMA((8,)),
             pltpu.SemaphoreType.DMA,
             pltpu.SemaphoreType.DMA((4,)),
             pltpu.SemaphoreType.DMA((4,)),

time: 41.5 us -> 40 us (0.964)
  Pallas kernels: 39.6 us -> 38 us
    pallas_call x1, Pallas kernels: 39.6 us -> 38 us  [shards(): pl.pallas_call(kernel, out_shape=jax.ShapeDtypeStruct(wafer_state.shape,...]
where the time goes in v4:
time: 40 us; the launch traced here: 39.8 us
  Pallas kernels  38 us (95%)
  local copies, waits for them, and re-layouts  1.77 us (4%)
    pallas_call x1, Pallas kernels, shards(): pl.pallas_call(kernel, out_shape=jax.ShapeDtypeStruct(wafer_state.shape,...  38 us
    unnamed x1, local copies, waits for them, and re-layouts  1.77 us

profile of v4, /device:TPU:24, one launch (start us, length us, event | category | flops | bytes accessed | tf_op | source)
XLA Modules:
  0.0 39.8 jit_solution(1043604192834035004)
XLA Ops:
  0.0 38.0 %shard_map.55 = f32[16,16,384]{2,1,0:T(8,128)} custom-call(f32[512]{0:T(512)} %profile_ref.1, s32[4]{0:T(128)} %start_ref.1, s32[4]{0:T(128)} %steps_ref.1, f32[256]{0:T(256)} %coef_ref.1, f32[16,16,384]{2,1,0:T(8,128)} %x_ref.1), custom_call_target="tpu_custom_call" | custom-call | tf_op jit(solution)/shard_map/pallas_call | solution.py:455
  38.1 1.8 %copy.7 = f32[16,16,384]{2,1,0:T(8,128)} copy(f32[16,16,384]{2,1,0:T(8,128)} %shard_map.55) | data formatting | bytes 786432

commit v5 on v4

--- a/solution.py
+++ b/solution.py
@@ -82,9 +82,10 @@
 
     def halo_copy(ds, dc, part=0):
         if ds == 0:
-            k = sides.index((ds, dc))
-            source_ref = x_ref.at[:, span(dc, cols, True, HALO), :]
-            landing = land.at[pl.ds(REACH, rows), span(dc, cols, False, HALO), :]
+            k = sides.index((ds, dc)) + 8 * part
+            half = rows // 2
+            source_ref = x_ref.at[pl.ds(half * part, half), span(dc, cols, True, HALO), :]
+            landing = land.at[pl.ds(REACH + half * part, half), span(dc, cols, False, HALO), :]
         else:
             k = (2 if ds < 0 else 5) + part
             if part == 0:
@@ -338,13 +339,14 @@
 
     lax.fori_loop(0, rows + 2 * REACH, margins, 0)
 
-    def arrive(ds, dc):
-        for part in range(3 if dc == 0 else 1):
+    def arrive(ds, dc, parts=(0, 1, 2)):
+        for part in parts:
             guarded(dc, halo_copy(-ds, -dc, part).wait_recv)
 
     pl.semaphore_wait(barrier, 3 + jnp.where(c > 0, 1, 0) + jnp.where(c < n_cross - 1, 1, 0))
-    for dc in (-1, 1):
-        guarded(dc, halo_copy(0, dc).start)
+    for part in range(2):
+        for dc in (-1, 1):
+            guarded(dc, halo_copy(0, dc, part).start)
     for ds in (-1, 1):
         halo_copy(ds, 0).start()
     own.wait()
@@ -408,21 +410,25 @@
         unpack(4 * part, 4)
         out_copy(part).start()
 
-    for dc in (-1, 1):
-        arrive(0, dc)
-    for ds in (-1, 1):
+    for n, ds in enumerate((-1, 1)):
+        for dc in (-1, 1):
+            arrive(0, dc, (n,))
         for part in (1, 2):
             halo_copy(ds, 0, part).start()
-    init_rows(0, rows)
+        init_rows(n * (rows // 2), rows // 2)
     middle(0, rows)
-    arrive(-1, 0)
-    init_rows(-REACH, REACH)
-    flank(0, -REACH, 1)
-    give(0)
-    arrive(1, 0)
-    init_rows(rows, REACH)
-    flank(0, rows, -1)
-    give(1)
+
+    def opening(n, carry):
+        pl.when(n == 0)(lambda: arrive(-1, 0))
+        pl.when(n == 1)(lambda: arrive(1, 0))
+        first = jnp.where(n == 0, -REACH, rows)
+        init_rows(first, REACH)
+        flank(0, first, jnp.where(n == 0, 1, -1))
+        pl.when(n == 0)(lambda: give(0))
+        pl.when(n == 1)(lambda: give(1))
+        return carry
+
+    lax.fori_loop(0, 2, opening, 0)
     middle(REACH, rows - 4)
     finish(1)
 
@@ -442,7 +448,7 @@
         for copy in mid_copies(side):
             copy.wait_send()
     for ds, dc in sides:
-        for part in range(3 if dc == 0 else 1):
+        for part in range(3 if dc == 0 else 2):
             guarded(dc, halo_copy(ds, dc, part).wait_send)
 
 
@@ -475,8 +481,8 @@
             pltpu.VMEM((X, 8, 128), f32),
             pltpu.VMEM((LEVELS * 24, 128), f32),
             pltpu.VMEM((2, Y, 128), f32),
-            pltpu.SemaphoreType.DMA((8,)),
-            pltpu.SemaphoreType.DMA((8,)),
+            pltpu.SemaphoreType.DMA((10,)),
+            pltpu.SemaphoreType.DMA((10,)),
             pltpu.SemaphoreType.DMA,
             pltpu.SemaphoreType.DMA((4,)),
             pltpu.SemaphoreType.DMA((4,)),

time: 40 us -> 39.4 us (0.985)
  Pallas kernels: 38 us -> 37.4 us
    pallas_call x1, Pallas kernels: 38 us -> 37.4 us  [shards(): pl.pallas_call(kernel, out_shape=jax.ShapeDtypeStruct(wafer_state.shape,...]
where the time goes in v5:
time: 39.4 us; the launch traced here: 39.2 us
  Pallas kernels  37.4 us (95%)
  local copies, waits for them, and re-layouts  1.77 us (4%)
    pallas_call x1, Pallas kernels, shards(): pl.pallas_call(kernel, out_shape=jax.ShapeDtypeStruct(wafer_state.shape,...  37.4 us
    unnamed x1, local copies, waits for them, and re-layouts  1.77 us

profile of v5, /device:TPU:24, one launch (start us, length us, event | category | flops | bytes accessed | tf_op | source)
XLA Modules:
  0.0 39.2 jit_solution(17795814396283918600)
XLA Ops:
  0.0 37.4 %shard_map.55 = f32[16,16,384]{2,1,0:T(8,128)} custom-call(f32[512]{0:T(512)} %profile_ref.1, s32[4]{0:T(128)} %start_ref.1, s32[4]{0:T(128)} %steps_ref.1, f32[256]{0:T(256)} %coef_ref.1, f32[16,16,384]{2,1,0:T(8,128)} %x_ref.1), custom_call_target="tpu_custom_call" | custom-call | tf_op jit(solution)/shard_map/pallas_call | solution.py:461
  37.5 1.8 %copy.7 = f32[16,16,384]{2,1,0:T(8,128)} copy(f32[16,16,384]{2,1,0:T(8,128)} %shard_map.55) | data formatting | bytes 786432
